TPU v7x, 32 devices: a whole 2x2x4 slice. The times are simulated.
32 devices in a mesh: occ: 4 (over y, core), vir: 8 (over z, x).
Axes of the slice: x: 2, y: 2, z: 4, core: 2. Of those that a mesh axis runs over, the one named last changes fastest.
Arguments:
- amplitudes: bfloat16 [32, 16, 128, 128], P(('occ', 'vir')), may hold values from -6 to 6
- amp_slots: int32 [32, 16], P(('occ', 'vir')), may hold values from 0 to 7, as said below
- integrals: bfloat16 [64, 48, 128, 128], P('vir', 'occ'), may hold values from -0.15625 to 0.15625
- int_columns: int32 [64, 48], replicated, may hold values from 0 to 63, as said below
- slot_tile: int32 [64], replicated, may hold values from 0 to 63, each once
Outputs:
- residual: bfloat16 [32, 16, 128, 128], P(('occ', 'vir'))
Inputs may be any that keep to these rules, and one draw needn't show every extreme that they name: `amp_slots`: within each group of 2 consecutive slots of a row the values are distinct. `int_columns`: the 48 entries of a row are distinct.
All inputs are finite; a program needn't handle non-finite values.
Results may differ from a plain program's by a relative error of at most 0.012.
Values may be sent and summed in bfloat16 or wider, within the bound.
A program may use at most 192 MiB of HBM per device.

v0:
```python
import jax
import jax.numpy as jnp
from jax import lax
from jax.sharding import PartitionSpec as P


def body(amplitudes, amp_slots, integrals, int_columns, slot_tile):
    rows_per_owner, slot_count, current_tile, unused_value = amplitudes.shape
    virtual_count = lax.axis_size("vir")
    row_groupings = slot_count // virtual_count
    vt_dev = integrals.shape[0]
    rows_of_group = rows_per_owner * virtual_count
    vir_pos = lax.axis_index("vir")
    all_slots = lax.all_gather(amp_slots, "vir", axis=0, tiled=True)
    table = slot_tile.reshape(virtual_count, vt_dev)
    slot_grid = all_slots.reshape(rows_of_group, virtual_count, row_groupings)
    matches_tab = slot_grid[..., None] == jnp.arange(vt_dev, dtype=jnp.int32)
    tile_identifiers = jnp.sum(jnp.where(matches_tab, table[None, :, None, :], 0), axis=-1)
    tile_identifiers = tile_identifiers.reshape(rows_of_group, slot_count)
    grouped = amplitudes.reshape(
        rows_per_owner, virtual_count, row_groupings, current_tile, current_tile
    )
    owned_amps = lax.all_to_all(grouped, "vir", split_axis=1, concat_axis=0, tiled=True)
    owned_amps = owned_amps.reshape(rows_of_group, row_groupings, current_tile, current_tile)
    own_ints = lax.all_gather(integrals, "occ", axis=1, tiled=True)
    own_cols = lax.dynamic_slice_in_dim(int_columns, vir_pos * vt_dev, vt_dev, 0)
    own_slots = lax.dynamic_slice_in_dim(all_slots, vir_pos * row_groupings, row_groupings, 1)

    def row_term(triple):
        amps_row, slots_row, ids_row = triple
        picked = jnp.take(own_ints, slots_row, axis=0)
        columns = jnp.take(own_cols, slots_row, axis=0)
        matches = columns[:, :, None] == ids_row[None, None, :]
        prods = jnp.einsum("kpq,kjqt->kjpt", amps_row, picked, preferred_element_type=jnp.float32)
        summed = jnp.einsum(
            "kjs,kjpt->spt", matches.astype(jnp.float32), prods, precision=lax.Precision.HIGHEST
        )
        return summed.astype(jnp.bfloat16)

    summed = lax.psum_scatter(
        lax.optimization_barrier(lax.map(row_term, (owned_amps, own_slots, tile_identifiers)))
        .astype(jnp.float32)
        .astype(jnp.bfloat16),
        "vir",
        scatter_dimension=0,
        tiled=True,
    ).astype(jnp.float32)
    return summed.astype(jnp.bfloat16)


def solution(mesh):
    in_specs = (
        P(("occ", "vir"), None, None, None),
        P(("occ", "vir"), None),
        P("vir", "occ", None, None),
        P(),
        P(),
    )
    out_specs = P(("occ", "vir"), None, None, None)
    return jax.shard_map(body, mesh=mesh, in_specs=in_specs, out_specs=out_specs, check_vma=False)
```

profile of v0, /device:TPU:0, one launch (start us, length us, event | category | flops | bytes accessed | tf_op | source)
XLA Modules:
  0.0 386.5 jit_solution(9607157665089281101)
XLA Ops:
  7.3 7.3 %all-to-all-start = ((bf16[1,8,2,128,128]{4,3,2,0,1:T(8,128)(2,1)}), bf16[1,8,2,128,128]{4,3,2,0,1:T(8,128)(2,1)S(1)}, u32[]{:S(2)}, u32[]{:S(2)}) async-start(bf16[1,8,2,128,128]{4,3,2,0,1:T(8,128)(2,1)} %bitcast.60), calls=%async_computation | async-start | bytes 1048576 | tf_op jit(solution)/shard_map/all_to_all | solution.py:23
  14.6 23.1 %all-gather = s32[8,1,16]{2,1,0:T(1,128)S(1)} all-gather(s32[1,1,16]{2,1,0:T(1,128)S(1)} %bitcast.64), channel_id=1, replica_groups=mesh['occ'=4,'vir'=8] {'vir'}, dimensions={0}, use_global_device_ids=true | all-gather | bytes 576 | tf_op jit(solution)/shard_map/all_gather | solution.py:14
  38.7 55.0 %all-gather.3.cloned.1.call-done = bf16[8,48,128,128]{3,2,1,0:T(8,128)(2,1)} async-done(((bf16[8,12,128,128]{3,2,1,0:T(8,128)(2,1)}), bf16[8,48,128,128]{3,2,1,0:T(8,128)(2,1)}) %all-gather.3.cloned.1.call-update) | async-done | bytes 12582928 | tf_op jit(solution)/shard_map/all_gather | solution.py:25
  93.7 191.7 %while.10 = (s32[]{:T(128)}, bf16[8,16,128,128]{3,1,2,0:T(8,128)(2,1)}, s32[8,2]{1,0:T(8,128)S(1)}, s32[8,48]{1,0:T(8,128)S(1)}, s32[8,16]{1,0:T(8,128)S(1)}, /*...) while((s32[]{:T(128)}, bf16[8,16,128,128]{3,1,2,0:T(8,128)(2,1)}, ...), condition=%wide.region_2.3_spmd, body=%wide.region_1.2_spmd.sunk | while | flops 706480768 | bytes 39393564 | solution.py:41
  94.6 5.7 %gather_fusion = bf16[2,48,128,128]{3,2,1,0:T(8,128)(2,1)S(1)} fusion(bf16[8,48,128,128]{3,2,1,0:T(8,128)(2,1)} %get-tuple-element.142, s32[1024]{0:T(1024)S(1)} %pad_clamp_fusion.2), kind=kCustom, calls=%fused_computation.1.clone.1 | custom fusion | bytes 6291464 | tf_op jit(solution)/shard_map/while/body/eval_jaxpr/jit(_take)/gather | solution.py:31
  105.2 6.7 %copy.36 = f32[2,48,128,128]{3,1,0,2:T(8,128)} copy(f32[2,48,128,128]{2,3,1,0:T(8,128)} %fusion.34) | data formatting | bytes 12582912 | tf_op jit(solution)/shard_map/while/body/eval_jaxpr/kpq,kjqt->kjpt/transpose | solution.py:34
  111.9 5.8 %fusion.36 = bf16[8,16,128,128]{3,1,2,0:T(8,128)(2,1)} fusion(bf16[8,16,128,128]{3,1,2,0:T(8,128)(2,1)} %get-tuple-element.130, s32[]{:T(128)S(6)} %copy.40, f32[2,48,128,128]{3,1,0,2:T(8,128)} %copy.36, s32[2,48]{1,0:T(2,128)S(1)} %broadcast_select_fusion.2, s32[16]{0:T(128)S(1)} %fusion.35), kind=kOutput, calls=%fused_computation.10.clone.1 | convolution fusion | flops 302253568 | bytes 6816196 | tf_op jit(solution)/shard_map/while/body/eval_jaxpr/kjs,kjpt->spt/dot_general | solution.py:35
  129.2 6.7 %copy.36 = f32[2,48,128,128]{3,1,0,2:T(8,128)} copy(f32[2,48,128,128]{2,3,1,0:T(8,128)} %fusion.34) | data formatting | bytes 12582912 | tf_op jit(solution)/shard_map/while/body/eval_jaxpr/kpq,kjqt->kjpt/transpose | solution.py:34
  135.9 5.8 %fusion.36 = bf16[8,16,128,128]{3,1,2,0:T(8,128)(2,1)} fusion(bf16[8,16,128,128]{3,1,2,0:T(8,128)(2,1)} %get-tuple-element.130, s32[]{:T(128)S(6)} %copy.40, f32[2,48,128,128]{3,1,0,2:T(8,128)} %copy.36, s32[2,48]{1,0:T(2,128)S(1)} %broadcast_select_fusion.2, s32[16]{0:T(128)S(1)} %fusion.35), kind=kOutput, calls=%fused_computation.10.clone.1 | convolution fusion | flops 302253568 | bytes 6816196 | tf_op jit(solution)/shard_map/while/body/eval_jaxpr/kjs,kjpt->spt/dot_general | solution.py:35
  142.6 5.7 %gather_fusion = bf16[2,48,128,128]{3,2,1,0:T(8,128)(2,1)S(1)} fusion(bf16[8,48,128,128]{3,2,1,0:T(8,128)(2,1)} %get-tuple-element.142, s32[1024]{0:T(1024)S(1)} %pad_clamp_fusion.2), kind=kCustom, calls=%fused_computation.1.clone.1 | custom fusion | bytes 6291464 | tf_op jit(solution)/shard_map/while/body/eval_jaxpr/jit(_take)/gather | solution.py:31
  153.2 6.7 %copy.36 = f32[2,48,128,128]{3,1,0,2:T(8,128)} copy(f32[2,48,128,128]{2,3,1,0:T(8,128)} %fusion.34) | data formatting | bytes 12582912 | tf_op jit(solution)/shard_map/while/body/eval_jaxpr/kpq,kjqt->kjpt/transpose | solution.py:34
  159.9 5.8 %fusion.36 = bf16[8,16,128,128]{3,1,2,0:T(8,128)(2,1)} fusion(bf16[8,16,128,128]{3,1,2,0:T(8,128)(2,1)} %get-tuple-element.130, s32[]{:T(128)S(6)} %copy.40, f32[2,48,128,128]{3,1,0,2:T(8,128)} %copy.36, s32[2,48]{1,0:T(2,128)S(1)} %broadcast_select_fusion.2, s32[16]{0:T(128)S(1)} %fusion.35), kind=kOutput, calls=%fused_computation.10.clone.1 | convolution fusion | flops 302253568 | bytes 6816196 | tf_op jit(solution)/shard_map/while/body/eval_jaxpr/kjs,kjpt->spt/dot_general | solution.py:35
  166.5 5.7 %gather_fusion = bf16[2,48,128,128]{3,2,1,0:T(8,128)(2,1)S(1)} fusion(bf16[8,48,128,128]{3,2,1,0:T(8,128)(2,1)} %get-tuple-element.142, s32[1024]{0:T(1024)S(1)} %pad_clamp_fusion.2), kind=kCustom, calls=%fused_computation.1.clone.1 | custom fusion | bytes 6291464 | tf_op jit(solution)/shard_map/while/body/eval_jaxpr/jit(_take)/gather | solution.py:31
  177.2 6.7 %copy.36 = f32[2,48,128,128]{3,1,0,2:T(8,128)} copy(f32[2,48,128,128]{2,3,1,0:T(8,128)} %fusion.34) | data formatting | bytes 12582912 | tf_op jit(solution)/shard_map/while/body/eval_jaxpr/kpq,kjqt->kjpt/transpose | solution.py:34
  183.8 5.8 %fusion.36 = bf16[8,16,128,128]{3,1,2,0:T(8,128)(2,1)} fusion(bf16[8,16,128,128]{3,1,2,0:T(8,128)(2,1)} %get-tuple-element.130, s32[]{:T(128)S(6)} %copy.40, f32[2,48,128,128]{3,1,0,2:T(8,128)} %copy.36, s32[2,48]{1,0:T(2,128)S(1)} %broadcast_select_fusion.2, s32[16]{0:T(128)S(1)} %fusion.35), kind=kOutput, calls=%fused_computation.10.clone.1 | convolution fusion | flops 302253568 | bytes 6816196 | tf_op jit(solution)/shard_map/while/body/eval_jaxpr/kjs,kjpt->spt/dot_general | solution.py:35
  201.1 6.7 %copy.36 = f32[2,48,128,128]{3,1,0,2:T(8,128)} copy(f32[2,48,128,128]{2,3,1,0:T(8,128)} %fusion.34) | data formatting | bytes 12582912 | tf_op jit(solution)/shard_map/while/body/eval_jaxpr/kpq,kjqt->kjpt/transpose | solution.py:34
  207.8 5.8 %fusion.36 = bf16[8,16,128,128]{3,1,2,0:T(8,128)(2,1)} fusion(bf16[8,16,128,128]{3,1,2,0:T(8,128)(2,1)} %get-tuple-element.130, s32[]{:T(128)S(6)} %copy.40, f32[2,48,128,128]{3,1,0,2:T(8,128)} %copy.36, s32[2,48]{1,0:T(2,128)S(1)} %broadcast_select_fusion.2, s32[16]{0:T(128)S(1)} %fusion.35), kind=kOutput, calls=%fused_computation.10.clone.1 | convolution fusion | flops 302253568 | bytes 6816196 | tf_op jit(solution)/shard_map/while/body/eval_jaxpr/kjs,kjpt->spt/dot_general | solution.py:35
  225.1 6.7 %copy.36 = f32[2,48,128,128]{3,1,0,2:T(8,128)} copy(f32[2,48,128,128]{2,3,1,0:T(8,128)} %fusion.34) | data formatting | bytes 12582912 | tf_op jit(solution)/shard_map/while/body/eval_jaxpr/kpq,kjqt->kjpt/transpose | solution.py:34
  231.7 5.8 %fusion.36 = bf16[8,16,128,128]{3,1,2,0:T(8,128)(2,1)} fusion(bf16[8,16,128,128]{3,1,2,0:T(8,128)(2,1)} %get-tuple-element.130, s32[]{:T(128)S(6)} %copy.40, f32[2,48,128,128]{3,1,0,2:T(8,128)} %copy.36, s32[2,48]{1,0:T(2,128)S(1)} %broadcast_select_fusion.2, s32[16]{0:T(128)S(1)} %fusion.35), kind=kOutput, calls=%fused_computation.10.clone.1 | convolution fusion | flops 302253568 | bytes 6816196 | tf_op jit(solution)/shard_map/while/body/eval_jaxpr/kjs,kjpt->spt/dot_general | solution.py:35
  249.0 6.7 %copy.36 = f32[2,48,128,128]{3,1,0,2:T(8,128)} copy(f32[2,48,128,128]{2,3,1,0:T(8,128)} %fusion.34) | data formatting | bytes 12582912 | tf_op jit(solution)/shard_map/while/body/eval_jaxpr/kpq,kjqt->kjpt/transpose | solution.py:34
  255.7 5.8 %fusion.36 = bf16[8,16,128,128]{3,1,2,0:T(8,128)(2,1)} fusion(bf16[8,16,128,128]{3,1,2,0:T(8,128)(2,1)} %get-tuple-element.130, s32[]{:T(128)S(6)} %copy.40, f32[2,48,128,128]{3,1,0,2:T(8,128)} %copy.36, s32[2,48]{1,0:T(2,128)S(1)} %broadcast_select_fusion.2, s32[16]{0:T(128)S(1)} %fusion.35), kind=kOutput, calls=%fused_computation.10.clone.1 | convolution fusion | flops 302253568 | bytes 6816196 | tf_op jit(solution)/shard_map/while/body/eval_jaxpr/kjs,kjpt->spt/dot_general | solution.py:35
  272.9 6.7 %copy.36 = f32[2,48,128,128]{3,1,0,2:T(8,128)} copy(f32[2,48,128,128]{2,3,1,0:T(8,128)} %fusion.34) | data formatting | bytes 12582912 | tf_op jit(solution)/shard_map/while/body/eval_jaxpr/kpq,kjqt->kjpt/transpose | solution.py:34
  279.6 5.8 %fusion.36 = bf16[8,16,128,128]{3,1,2,0:T(8,128)(2,1)} fusion(bf16[8,16,128,128]{3,1,2,0:T(8,128)(2,1)} %get-tuple-element.130, s32[]{:T(128)S(6)} %copy.40, f32[2,48,128,128]{3,1,0,2:T(8,128)} %copy.36, s32[2,48]{1,0:T(2,128)S(1)} %broadcast_select_fusion.2, s32[16]{0:T(128)S(1)} %fusion.35), kind=kOutput, calls=%fused_computation.10.clone.1 | convolution fusion | flops 302253568 | bytes 6816196 | tf_op jit(solution)/shard_map/while/body/eval_jaxpr/kjs,kjpt->spt/dot_general | solution.py:35
  290.7 88.9 %reduce-scatter.2.cloned.1.call-done = bf16[1,16,128,128]{3,2,1,0:T(8,128)(2,1)} async-done(((bf16[8,16,128,128]{3,2,1,0:T(8,128)(2,1)}), bf16[1,16,128,128]{3,2,1,0:T(8,128)(2,1)}) %reduce-scatter.2.cloned.1.call-update) | async-done | bytes 524304 | tf_op jit(solution)/shard_map/reduce_scatter | solution.py:40
  (115 shorter events, 81.6 us)
Async XLA Ops:
  6.5 32.0 %copy-start = (s32[64,48]{0,1:T(8,128)S(1)}, s32[64,48]{0,1:T(8,128)}, u32[]{:S(2)}) copy-start(s32[64,48]{0,1:T(8,128)} %param.10) | copy-start | bytes 36868
  6.5 8.1 %copy-start.3 = (s32[1,16]{1,0:T(1,128)S(1)}, s32[1,16]{1,0:T(1,128)}, u32[]{:S(2)}) copy-start(s32[1,16]{1,0:T(1,128)} %param.8) | copy-start | bytes 196
  6.5 31.3 %copy-start.4 = (s32[64]{0:T(128)S(1)}, s32[64]{0:T(128)}, u32[]{:S(2)}) copy-start(s32[64]{0:T(128)} %param.11) | copy-start | bytes 772
  6.5 87.2 %all-gather.3.cloned.1.call-start = ((), (), s32[]{:S(2)}) async-start(), calls=%async_computation.2 | async-start | bytes 15728640 | tf_op jit(solution)/shard_map/all_gather | solution.py:25
  7.3 31.5 %all-to-all-start = ((bf16[1,8,2,128,128]{4,3,2,0,1:T(8,128)(2,1)}), bf16[1,8,2,128,128]{4,3,2,0,1:T(8,128)(2,1)S(1)}, u32[]{:S(2)}, u32[]{:S(2)}) async-start(bf16[1,8,2,128,128]{4,3,2,0,1:T(8,128)(2,1)} %bitcast.60), calls=%async_computation | async-start | bytes 1048576 | tf_op jit(solution)/shard_map/all_to_all | solution.py:23
  14.6 365.1 %reduce-scatter.2.cloned.1.call-start = ((), (), s32[]{:S(2)}) async-start(), calls=%async_computation.3 | async-start | bytes 4718592 | tf_op jit(solution)/shard_map/reduce_scatter | solution.py:40
  93.7 0.8 copy-start.1
  111.9 5.8 %copy-start.2 = (bf16[8,2,128,128]{3,2,1,0:T(8,128)(2,1)S(1)}, bf16[8,2,128,128]{3,2,1,0:T(8,128)(2,1)}, u32[]{:S(2)}) copy-start(bf16[8,2,128,128]{3,2,1,0:T(8,128)(2,1)} %copy-done.1) | copy-start | bytes 1572868 | tf_op jit(solution)/shard_map/while
  117.7 0.8 copy-start.1
  135.9 5.8 %copy-start.2 = (bf16[8,2,128,128]{3,2,1,0:T(8,128)(2,1)S(1)}, bf16[8,2,128,128]{3,2,1,0:T(8,128)(2,1)}, u32[]{:S(2)}) copy-start(bf16[8,2,128,128]{3,2,1,0:T(8,128)(2,1)} %copy-done.1) | copy-start | bytes 1572868 | tf_op jit(solution)/shard_map/while
  141.7 0.8 copy-start.1
  159.9 5.8 %copy-start.2 = (bf16[8,2,128,128]{3,2,1,0:T(8,128)(2,1)S(1)}, bf16[8,2,128,128]{3,2,1,0:T(8,128)(2,1)}, u32[]{:S(2)}) copy-start(bf16[8,2,128,128]{3,2,1,0:T(8,128)(2,1)} %copy-done.1) | copy-start | bytes 1572868 | tf_op jit(solution)/shard_map/while
  165.7 0.8 copy-start.1
  183.8 5.8 %copy-start.2 = (bf16[8,2,128,128]{3,2,1,0:T(8,128)(2,1)S(1)}, bf16[8,2,128,128]{3,2,1,0:T(8,128)(2,1)}, u32[]{:S(2)}) copy-start(bf16[8,2,128,128]{3,2,1,0:T(8,128)(2,1)} %copy-done.1) | copy-start | bytes 1572868 | tf_op jit(solution)/shard_map/while
  189.6 0.8 copy-start.1
  207.8 5.8 %copy-start.2 = (bf16[8,2,128,128]{3,2,1,0:T(8,128)(2,1)S(1)}, bf16[8,2,128,128]{3,2,1,0:T(8,128)(2,1)}, u32[]{:S(2)}) copy-start(bf16[8,2,128,128]{3,2,1,0:T(8,128)(2,1)} %copy-done.1) | copy-start | bytes 1572868 | tf_op jit(solution)/shard_map/while
  213.6 0.8 copy-start.1
  231.7 5.8 %copy-start.2 = (bf16[8,2,128,128]{3,2,1,0:T(8,128)(2,1)S(1)}, bf16[8,2,128,128]{3,2,1,0:T(8,128)(2,1)}, u32[]{:S(2)}) copy-start(bf16[8,2,128,128]{3,2,1,0:T(8,128)(2,1)} %copy-done.1) | copy-start | bytes 1572868 | tf_op jit(solution)/shard_map/while
  237.5 0.8 copy-start.1
  255.7 5.8 %copy-start.2 = (bf16[8,2,128,128]{3,2,1,0:T(8,128)(2,1)S(1)}, bf16[8,2,128,128]{3,2,1,0:T(8,128)(2,1)}, u32[]{:S(2)}) copy-start(bf16[8,2,128,128]{3,2,1,0:T(8,128)(2,1)} %copy-done.1) | copy-start | bytes 1572868 | tf_op jit(solution)/shard_map/while
  261.5 0.8 copy-start.1
  279.6 5.8 %copy-start.2 = (bf16[8,2,128,128]{3,2,1,0:T(8,128)(2,1)S(1)}, bf16[8,2,128,128]{3,2,1,0:T(8,128)(2,1)}, u32[]{:S(2)}) copy-start(bf16[8,2,128,128]{3,2,1,0:T(8,128)(2,1)} %copy-done.1) | copy-start | bytes 1572868 | tf_op jit(solution)/shard_map/while
Sparse Core Ops, SparseCore 0:
  8.9 84.7 all-gather.2
  290.9 88.7 reduce-scatter.1
where the time goes:
time: 388 us; the launch traced here: 386 us
  waiting for transfers between devices  145 us (37%)
  local copies, waits for them, and re-layouts  111 us (29%)
  matrix products  85.5 us (22%)
  blocking collectives  23.1 us (6%)
  between operations  13.4 us (3%)
  starting transfers between devices  7.33 us (2%)
    reduce_scatter x1, waiting for transfers between devices, body(): lax.psum_scatter(lax.optimization_barrier(lax.map(row_term, (owned_amps,...  88.9 us
    all_gather x1, waiting for transfers between devices, body(): own_ints = lax.all_gather(integrals, 'occ', axis=1, tiled=True)  55 us
    transpose x8, local copies, waits for them, and re-layouts, row_term(): jnp.einsum('kpq,kjqt->kjpt', amps_row, picked, preferred_element_type=jnp...  53.4 us
    dot_general x8, matrix products, row_term(): jnp.einsum('kjs,kjpt->spt', matches.astype(jnp.float32), prods, precision...  46.4 us
    gather x8, local copies, waits for them, and re-layouts, row_term(): picked = jnp.take(own_ints, slots_row, axis=0)  45.8 us
    dot_general x8, matrix products, row_term(): jnp.einsum('kpq,kjqt->kjpt', amps_row, picked, preferred_element_type=jnp...  39.1 us
    all_gather x1, blocking collectives, body(): all_slots = lax.all_gather(amp_slots, 'vir', axis=0, tiled=True)  23.1 us
  transfers between devices with their start and end apart: 3, of which 2 were waited for; matrix products, arithmetic and copies ran while one was open for 0% of the time, Pallas kernels for 0%

commit v1 on v0

v1 whole, which is shorter than its diff:
```python
import functools

import jax
import jax.numpy as jnp
from jax import lax
from jax.experimental import pallas as pl
from jax.experimental.pallas import tpu as pltpu
from jax.sharding import PartitionSpec as P

MESH = pl.DeviceIdType.MESH
CORES = 2
CHUNKS = ((False, 0, 32), (False, 32, 32), (False, 64, 32), (False, 96, 32))


def jobs_of(ny, chunks):
    jobs = []
    for number, (spread, _, _) in enumerate(chunks):
        for step in range(ny if spread else 1):
            jobs.append((number, step))
    return jobs


def kernel(dims, chunks, jobs, amps, tables, ints, out, *scratch):
    ny, nz, nx, slots, tiles = dims
    nv, no = nz * nx, ny * CORES
    spread_any = any(c[0] for c in chunks)
    n_chunks, n_jobs = len(chunks), len(jobs)
    weights = scratch[:n_chunks]
    terms = scratch[n_chunks : n_chunks + n_jobs]
    from_x = scratch[n_chunks + n_jobs : n_chunks + 2 * n_jobs]
    from_z = scratch[n_chunks + 2 * n_jobs : n_chunks + 3 * n_jobs]
    from_y = scratch[n_chunks + 3 * n_jobs : n_chunks + 4 * n_jobs]
    amp_buf, tab_buf, tab_smem, send_sem, recv_sem, loc_sem = scratch[n_chunks + 4 * n_jobs :]

    occ, vir = lax.axis_index("occ"), lax.axis_index("vir")
    y, core = occ // CORES, lax.rem(occ, CORES)
    z, x = vir // nx, lax.rem(vir, nx)
    partner = y * CORES + (1 - core)

    def occ_at(step):
        return lax.rem(y + step, ny) * CORES + core

    counts = {"remote": 0, "local": 0}
    sent = []

    def remote(src, dst, where):
        at = counts["remote"]
        counts["remote"] += 1
        copy = pltpu.make_async_remote_copy(
            src_ref=src, dst_ref=dst, send_sem=send_sem.at[at], recv_sem=recv_sem.at[at],
            device_id=where, device_id_type=MESH,
        )
        copy.start()
        sent.append(copy)
        return copy

    def local(src, dst):
        at = counts["local"]
        counts["local"] += 1
        copy = pltpu.make_async_copy(src, dst, loc_sem.at[at])
        copy.start()
        return copy

    barrier = pltpu.get_barrier_semaphore()
    peers = [{"occ": occ, "vir": lax.rem(vir + d, nv)} for d in range(1, nv)]
    peers += [{"occ": occ_at(d), "vir": vir} for d in range(1, ny)]
    peers += [{"occ": partner, "vir": vir}]
    for peer in peers:
        pl.semaphore_signal(barrier, inc=1, device_id=peer, device_id_type=MESH)

    own_copies = {}

    def span(number, source):
        spread = chunks[number][0]
        first = (lax.rem(source, CORES) if spread else source) * tiles
        return weights[number].at[pl.ds(first, tiles)]

    def part(number):
        _, first, width = chunks[number]
        return ints.at[:, pl.ds(first, width), :]

    amp_own = local(amps.at[vir], amp_buf.at[0, vir])
    tab_own = local(tables.at[vir], tab_buf.at[0, vir])
    for number, (_, _, width) in enumerate(chunks):
        own_copies[number] = local(part(number), span(number, occ))
    for number, (spread, _, width) in enumerate(chunks):
        weights[number][(CORES if spread else no) * tiles] = jnp.zeros((width, 128), jnp.bfloat16)

    pl.semaphore_wait(barrier, len(peers))

    across, side = {}, {}

    def start_across(number):
        across[number] = [
            remote(part(number), span(number, occ), {"occ": occ_at(d), "vir": vir})
            for d in range(1, ny)
        ]

    def start_side(number):
        side[number] = [remote(part(number), span(number, occ), {"occ": partner, "vir": vir})]

    narrow = [c for c in range(n_chunks) if not chunks[c][0]]
    incoming = []
    for d in range(1, nv):
        to = lax.rem(vir + d, nv)
        incoming.append(remote(tables.at[to], tab_buf.at[0, vir], {"occ": occ, "vir": to}))
        incoming.append(remote(amps.at[to], amp_buf.at[0, vir], {"occ": occ, "vir": to}))
    start_across(narrow[0])
    for number in range(n_chunks):
        start_side(number)
    if not spread_any:
        for number in narrow[1:]:
            start_across(number)
    amp_own.wait()
    tab_own.wait()
    for copy in incoming:
        copy.wait_recv()
    others = []
    if spread_any:
        for d in range(1, ny):
            where = {"occ": occ_at(d), "vir": vir}
            others.append(
                (
                    remote(tab_buf.at[0], tab_buf.at[d], where),
                    remote(amp_buf.at[0], amp_buf.at[d], where),
                )
            )
        for number in narrow[1:]:
            start_across(number)
    tab_copy = local(tab_buf.at[0], tab_smem.at[0])
    tab_copy.wait()

    def gather(number):
        own_copies[number].wait()
        if not chunks[number][0]:
            for d in range(1, ny):
                across[number][d - 1].wait_recv()
                source = lax.rem(y - d + ny, ny) * CORES + core
                side[number].append(
                    remote(span(number, source), span(number, source), {"occ": partner, "vir": vir})
                )
        for copy in side[number]:
            copy.wait_recv()

    def compute(job, x_to):
        number, step = jobs[job]
        spread, _, width = chunks[number]
        weight, term = weights[number], terms[job]
        group = step
        per_slot = amp_buf.shape[2] // 128

        def row(z_to, carry):
            r = z_to * nx + x_to
            columns = []
            for k in range(per_slot):
                pieces = []
                for s in range(slots):
                    at = tab_smem[group, r, k, s]
                    if spread:
                        at = at - y * (CORES * tiles)
                        good = (at >= 0) & (at < CORES * tiles)
                        at = jnp.where(good, at, CORES * tiles)
                    pieces.append(weight[at])
                columns.append(jnp.concatenate(pieces, axis=0))
            left = jnp.concatenate(columns, axis=1)
            prod = jnp.dot(left, amp_buf[group, r], preferred_element_type=jnp.float32)
            term[x_to, z_to] = prod.astype(jnp.bfloat16).reshape(slots, width, 128)
            return carry

        lax.fori_loop(0, nz, row, 0)

    x_copies, z_copies, y_copies = {}, {}, {}

    def first_stage(job):
        x_copies[job] = []
        for d in range(1, nx):
            to = lax.rem(x + d, nx)
            compute(job, to)
            x_copies[job].append(
                remote(terms[job].at[to], from_x[job].at[d - 1], {"occ": occ, "vir": z * nx + to})
            )
        compute(job, x)

    def second_stage(job):
        for copy in x_copies[job]:
            copy.wait_recv()
        z_copies[job] = []
        for d in range(1, nz + 1):
            to = lax.rem(z + d, nz)
            total = terms[job][x, to].astype(jnp.float32)
            for e in range(nx - 1):
                total += from_x[job][e, to].astype(jnp.float32)
            terms[job][x, to] = total.astype(jnp.bfloat16)
            if d < nz:
                z_copies[job].append(
                    remote(
                        terms[job].at[x, to], from_z[job].at[d - 1],
                        {"occ": occ, "vir": to * nx + x},
                    )
                )

    def third_stage(job):
        number, step = jobs[job]
        spread, first, width = chunks[number]
        for copy in z_copies[job]:
            copy.wait_recv()
        total = terms[job][x, z].astype(jnp.float32)
        for e in range(nz - 1):
            total += from_z[job][e].astype(jnp.float32)
        if step > 0:
            terms[job][x, z] = total.astype(jnp.bfloat16)
            y_copies[job] = remote(
                terms[job].at[x, z], from_y[job], {"occ": occ_at(step), "vir": vir}
            )
            return
        for other in range(n_jobs):
            if jobs[other][0] == number and jobs[other][1] > 0:
                y_copies[other].wait_recv()
                total += from_y[other][...].astype(jnp.float32)
        out[:, pl.ds(first, width), :] = total.astype(jnp.bfloat16)

    if spread_any:
        order = [j for j in range(n_jobs) if jobs[j][1] == 0 and chunks[jobs[j][0]][0]]
        order += [j for j in range(n_jobs) if not chunks[jobs[j][0]][0]]
        late = [j for j in range(n_jobs) if jobs[j][1] > 0]
        order = order[:2] + late + order[2:]
    else:
        order = list(range(n_jobs))
    gathered = set()
    finals = []

    def flush(job):
        if chunks[jobs[job][0]][0] and jobs[job][1] == 0:
            finals.append(job)
        else:
            third_stage(job)

    previous = None
    for job in order:
        number, step = jobs[job]
        if number not in gathered:
            gathered.add(number)
            gather(number)
        if step > 0:
            for copy in others[step - 1]:
                copy.wait_recv()
            again = local(tab_buf.at[step], tab_smem.at[step])
            again.wait()
        first_stage(job)
        if previous is not None:
            flush(previous)
        second_stage(job)
        previous = job
    flush(previous)
    for job in finals:
        third_stage(job)
    for copy in sent:
        copy.wait_send()


def body(nx, amplitudes, amp_slots, integrals, int_columns, slot_tile):
    _, slots, tile, _ = amplitudes.shape
    nv, no = lax.axis_size("vir"), lax.axis_size("occ")
    ny, nz = no // CORES, nv // nx
    owned, share = integrals.shape[:2]
    tiles = owned * share
    per_owner = slots // nv
    chunks = CHUNKS if ny == 2 else tuple((False, first, width) for _, first, width in CHUNKS)
    jobs = jobs_of(ny, chunks)

    here = amp_slots[0]
    store = (jnp.arange(slots, dtype=jnp.int32) // per_owner) * owned + here
    hot = store[:, None] == jnp.arange(nv * owned, dtype=jnp.int32)[None, :]
    tile_id = jnp.sum(jnp.where(hot, slot_tile[None, :], 0), axis=1)
    columns = jnp.sum(jnp.where(hot[:, :, None], int_columns[None], 0), axis=1)
    entry = jnp.arange(share * no, dtype=jnp.int32)
    place = (entry // share) * tiles + entry % share
    match = columns[:, :, None] == tile_id[None, None, :]
    place = place[None, :, None] + (here * share)[:, None, None]
    table = jnp.min(jnp.where(match, place, no * tiles), axis=1)
    table = table.reshape(nv, per_owner, slots)
    table = jnp.pad(table, ((0, 0), (0, 8 - per_owner), (0, 128 - slots)))

    amps = jnp.swapaxes(amplitudes[0], 1, 2).reshape(nv, per_owner * tile, tile)
    ints = jnp.swapaxes(integrals, 2, 3).reshape(tiles, tile, tile)

    bf16 = jnp.bfloat16
    groups = ny if any(c[0] for c in chunks) else 1
    scratch = [
        pltpu.VMEM(((CORES if spread else no) * tiles + 1, width, tile), bf16)
        for spread, _, width in chunks
    ]
    widths = [chunks[number][2] for number, _ in jobs]
    scratch += [pltpu.VMEM((nx, nz, slots, w, tile), bf16) for w in widths]
    scratch += [pltpu.VMEM((nx - 1, nz, slots, w, tile), bf16) for w in widths]
    scratch += [pltpu.VMEM((nz - 1, slots, w, tile), bf16) for w in widths]
    scratch += [
        pltpu.VMEM((slots, w, tile) if step > 0 else (8, 128), bf16)
        for w, (_, step) in zip(widths, jobs)
    ]
    scratch += [
        pltpu.VMEM((groups, nv, per_owner * tile, tile), bf16),
        pltpu.VMEM((groups, nv, 8, 128), jnp.int32),
        pltpu.SMEM((groups, nv, 8, 128), jnp.int32),
        pltpu.SemaphoreType.DMA((128,)),
        pltpu.SemaphoreType.DMA((128,)),
        pltpu.SemaphoreType.DMA((16,)),
    ]
    result = pl.pallas_call(
        functools.partial(kernel, (ny, nz, nx, slots, tiles), chunks, jobs),
        out_shape=jax.ShapeDtypeStruct((slots, tile, tile), bf16),
        in_specs=[pl.BlockSpec(memory_space=pl.ANY)] * 3,
        out_specs=pl.BlockSpec(memory_space=pltpu.VMEM),
        scratch_shapes=scratch,
        compiler_params=pltpu.CompilerParams(
            collective_id=0, has_side_effects=True, vmem_limit_bytes=66_000_000
        ),
    )(amps, table, ints)
    return jnp.swapaxes(result, 1, 2)[None]


def solution(mesh):
    nv = mesh.shape["vir"]
    nx = nv // min(4, nv)
    in_specs = (
        P(("occ", "vir"), None, None, None),
        P(("occ", "vir"), None),
        P("vir", "occ", None, None),
        P(),
        P(),
    )
    out_specs = P(("occ", "vir"), None, None, None)
    return jax.shard_map(
        functools.partial(body, nx), mesh=mesh, in_specs=in_specs, out_specs=out_specs,
        check_vma=False,
    )
```

time: 388 us -> 118 us (0.30)
  waiting for transfers between devices: 145 us -> 0 us
  Pallas kernels: 0 us -> 105 us
  local copies, waits for them, and re-layouts: 111 us -> 9.33 us
  matrix products: 85.5 us -> 0 us
  blocking collectives: 23.1 us -> 0 us
  between operations: 13.4 us -> 0.02 us
  starting transfers between devices: 7.33 us -> 0 us
    pallas_call x0 -> x1, Pallas kernels: none -> 105 us  [body(): pl.pallas_call(functools.partial(kernel, (ny, nz, nx, slots, tiles), chun...]
    reduce_scatter x1 -> x0, waiting for transfers between devices: 88.9 us -> none  [body(): lax.psum_scatter(lax.optimization_barrier(lax.map(row_term, (owned_amps,...]
    dot_general x16 -> x0, matrix products: 85.5 us -> none  [the longest x8 46.4 us: row_term(): jnp.einsum('kjs,kjpt->spt', matches.astype(jnp.float32), prods, precision...]
    all_gather x1 -> x0, waiting for transfers between devices: 55 us -> none  [body(): own_ints = lax.all_gather(integrals, 'occ', axis=1, tiled=True)]
    gather x16 -> x0, local copies, waits for them, and re-layouts: 50.3 us -> none  [the longest x8 45.8 us: row_term(): picked = jnp.take(own_ints, slots_row, axis=0)]
    transpose x8 -> x2, local copies, waits for them, and re-layouts: 53.4 us -> 6.68 us  [the longest x1 4.64 us: body(): ints = jnp.swapaxes(integrals, 2, 3).reshape(tiles, tile, tile)]
    all_gather x1 -> x0, blocking collectives: 23.1 us -> none  [body(): all_slots = lax.all_gather(amp_slots, 'vir', axis=0, tiled=True)]
    all_to_all x1 -> x0, starting transfers between devices: 7.29 us -> none  [body(): lax.all_to_all(grouped, 'vir', split_axis=1, concat_axis=0, tiled=True)]
  transfers between devices with their start and end apart: 3 -> 0, of which waited for: 2 -> 0; matrix products, arithmetic and copies ran while one was open for 0% -> 0% of each run, Pallas kernels for 0% -> 0%
where the time goes in v1:
time: 118 us; the launch traced here: 117 us
  Pallas kernels  105 us (89%)
  local copies, waits for them, and re-layouts  9.33 us (8%)
  other arithmetic  3.15 us (3%)
    pallas_call x1, Pallas kernels, body(): pl.pallas_call(functools.partial(kernel, (ny, nz, nx, slots, tiles), chun...  105 us
    transpose x1, local copies, waits for them, and re-layouts, body(): ints = jnp.swapaxes(integrals, 2, 3).reshape(tiles, tile, tile)  4.64 us

profile of v1, /device:TPU:0, one launch (start us, length us, event | category | flops | bytes accessed | tf_op | source)
XLA Modules:
  0.0 117.0 jit_solution(14750557608338860572)
XLA Ops:
  0.0 0.7 fusion.2
  0.7 0.8 select_reduce_fusion.2
  1.5 0.1 iota_compare_fusion
  1.6 1.1 select_reduce_fusion
  2.7 0.1 broadcast_add_fusion
  2.7 0.4 select_reduce_fusion.1
  3.2 0.6 pad.4.tables
  3.8 2.0 %copy.10 = bf16[16,128,128]{2,1,0:T(8,128)(2,1)} copy(bf16[16,128,128]{1,2,0:T(8,128)(2,1)} %bitcast.17) | data formatting | bytes 1048576 | tf_op jit(solution)/shard_map/transpose | solution.py:284
  5.8 4.6 %copy.11 = bf16[8,12,128,128]{3,2,1,0:T(8,128)(2,1)} copy(bf16[8,12,128,128]{2,3,1,0:T(8,128)(2,1)} %bitcast.14) | data formatting | bytes 6291456 | tf_op jit(solution)/shard_map/transpose | solution.py:285
  10.5 104.5 %shard_map.55 = bf16[16,128,128]{2,1,0:T(8,128)(2,1)} custom-call(bf16[8,256,128]{2,1,0:T(8,128)(2,1)} %bitcast.16, s32[8,8,128]{2,1,0:T(8,128)} %pad.4.tables, bf16[96,128,128]{2,1,0:T(8,128)(2,1)} %bitcast.13), custom_call_target="tpu_custom_call" | custom-call | tf_op jit(solution)/shard_map/pallas_call | solution.py:309
  115.0 2.0 %copy.12 = bf16[1,16,128,128]{3,2,1,0:T(8,128)(2,1)} copy(bf16[1,16,128,128]{2,3,1,0:T(8,128)(2,1)} %bitcast.15) | data formatting | bytes 1048576 | tf_op jit(solution)/shard_map/broadcast_in_dim | solution.py:319
  (1 shorter events, 0.0 us)

commit v2 on v1

--- a/solution.py
+++ b/solution.py
@@ -9,7 +9,7 @@
 
 MESH = pl.DeviceIdType.MESH
 CORES = 2
-CHUNKS = ((False, 0, 32), (False, 32, 32), (False, 64, 32), (False, 96, 32))
+CHUNKS = ((False, 0, 32), (False, 32, 32), (False, 64, 32), (False, 96, 16), (False, 112, 16))
 
 
 def jobs_of(ny, chunks):
@@ -20,8 +20,9 @@
     return jobs
 
 
-def kernel(dims, chunks, jobs, amps, tables, ints, out, *scratch):
-    ny, nz, nx, slots, tiles = dims
+def kernel(dims, chunks, jobs, own_slots, slot_tile, columns_of, amps_in, ints, out, *scratch):
+    ny, nz, nx, slots, owned, share = dims
+    tiles = owned * share
     nv, no = nz * nx, ny * CORES
     spread_any = any(c[0] for c in chunks)
     n_chunks, n_jobs = len(chunks), len(jobs)
@@ -30,7 +31,7 @@
     from_x = scratch[n_chunks + n_jobs : n_chunks + 2 * n_jobs]
     from_z = scratch[n_chunks + 2 * n_jobs : n_chunks + 3 * n_jobs]
     from_y = scratch[n_chunks + 3 * n_jobs : n_chunks + 4 * n_jobs]
-    amp_buf, tab_buf, tab_smem, send_sem, recv_sem, loc_sem = scratch[n_chunks + 4 * n_jobs :]
+    raw_ints, raw_amps, amps, tables, amp_buf, tab_buf, tab_smem, send_sem, recv_sem, loc_sem = scratch[n_chunks + 4 * n_jobs :]
 
     occ, vir = lax.axis_index("occ"), lax.axis_index("vir")
     y, core = occ // CORES, lax.rem(occ, CORES)
@@ -68,49 +69,105 @@
     for peer in peers:
         pl.semaphore_signal(barrier, inc=1, device_id=peer, device_id_type=MESH)
 
-    own_copies = {}
+    held = raw_ints.shape[0] // share
+
+    def fetch(g):
+        return local(
+            ints.at[pl.ds(g * share, share)], raw_ints.at[pl.ds((g % held) * share, share)]
+        )
+
+    pieces_in = [fetch(g) for g in range(held)]
+    amps_copy = local(amps_in, raw_amps)
 
     def span(number, source):
         spread = chunks[number][0]
         first = (lax.rem(source, CORES) if spread else source) * tiles
         return weights[number].at[pl.ds(first, tiles)]
 
-    def part(number):
-        _, first, width = chunks[number]
-        return ints.at[:, pl.ds(first, width), :]
-
-    amp_own = local(amps.at[vir], amp_buf.at[0, vir])
-    tab_own = local(tables.at[vir], tab_buf.at[0, vir])
-    for number, (_, _, width) in enumerate(chunks):
-        own_copies[number] = local(part(number), span(number, occ))
     for number, (spread, _, width) in enumerate(chunks):
         weights[number][(CORES if spread else no) * tiles] = jnp.zeros((width, 128), jnp.bfloat16)
 
-    pl.semaphore_wait(barrier, len(peers))
+    def turn(slot, tile):
+        turned = raw_ints[slot].T
+        for number, (spread, first, width) in enumerate(chunks):
+            at = (core if spread else occ) * tiles + tile
+            weights[number][at] = turned[first : first + width]
 
     across, side = {}, {}
 
     def start_across(number):
         across[number] = [
-            remote(part(number), span(number, occ), {"occ": occ_at(d), "vir": vir})
+            remote(span(number, occ), span(number, occ), {"occ": occ_at(d), "vir": vir})
             for d in range(1, ny)
         ]
 
     def start_side(number):
-        side[number] = [remote(part(number), span(number, occ), {"occ": partner, "vir": vir})]
+        side[number] = [
+            remote(span(number, occ), span(number, occ), {"occ": partner, "vir": vir})
+        ]
 
     narrow = [c for c in range(n_chunks) if not chunks[c][0]]
+    lead = narrow[0]
+    across[lead] = []
+
+    def start_lead(g):
+        piece = weights[lead].at[pl.ds(occ * tiles + g * share, share)]
+        for d in range(1, ny):
+            across[lead].append(remote(piece, piece, {"occ": occ_at(d), "vir": vir}))
+
+    for g in range(owned):
+        pieces_in[g].wait()
+
+        @pl.loop(0, share)
+        def _(j, g=g):
+            turn((g % held) * share + j, g * share + j)
+
+        if g + held < owned:
+            pieces_in.append(fetch(g + held))
+
+        if g == 0:
+            pl.semaphore_wait(barrier, len(peers))
+        else:
+            start_lead(g - 1)
+    start_lead(owned - 1)
+
+    if not spread_any:
+        for number in narrow[1:]:
+            start_across(number)
+
+    nv_slots = slots // nv
+    rows = lax.broadcasted_iota(jnp.int32, (slots, share * no), 0)
+    entry = lax.broadcasted_iota(jnp.int32, (slots, share * no), 1)
+    place = (entry // share) * tiles + lax.rem(entry, share)
+    wanted = jnp.zeros((slots, share * no), jnp.int32)
+    for s in range(slots):
+        wanted = jnp.where(rows == s, slot_tile[(s // nv_slots) * owned + own_slots[0, s]], wanted)
+    lanes = lax.broadcasted_iota(jnp.int32, (slots, 128), 1)
+    for v in range(nv):
+        mapped = jnp.zeros((slots, 128), jnp.int32)
+        for k in range(nv_slots):
+            mine = own_slots[0, v * nv_slots + k]
+            reached = columns_of[pl.ds(v * owned + mine, 1), :]
+            found = jnp.where(reached == wanted, place + mine * share, no * tiles)
+            mapped = jnp.where(lanes == k, jnp.min(found, axis=1, keepdims=True), mapped)
+        tables[v] = mapped
+
+    amps_copy.wait()
+
+    @pl.loop(0, slots)
+    def _(s):
+        at = pl.ds(pl.multiple_of(lax.rem(s, nv_slots) * 128, 128), 128)
+        amps[s // nv_slots, at, :] = raw_amps[s].T
+
+    tab_own = local(tables.at[vir], tab_buf.at[0, vir])
+    amp_own = local(amps.at[vir], amp_buf.at[0, vir])
     incoming = []
     for d in range(1, nv):
         to = lax.rem(vir + d, nv)
         incoming.append(remote(tables.at[to], tab_buf.at[0, vir], {"occ": occ, "vir": to}))
         incoming.append(remote(amps.at[to], amp_buf.at[0, vir], {"occ": occ, "vir": to}))
-    start_across(narrow[0])
     for number in range(n_chunks):
         start_side(number)
-    if not spread_any:
-        for number in narrow[1:]:
-            start_across(number)
     amp_own.wait()
     tab_own.wait()
     for copy in incoming:
@@ -131,10 +188,13 @@
     tab_copy.wait()
 
     def gather(number):
-        own_copies[number].wait()
         if not chunks[number][0]:
             for d in range(1, ny):
-                across[number][d - 1].wait_recv()
+                if number == lead:
+                    for g in range(owned):
+                        across[number][g * (ny - 1) + d - 1].wait_recv()
+                else:
+                    across[number][d - 1].wait_recv()
                 source = lax.rem(y - d + ny, ny) * CORES + core
                 side[number].append(
                     remote(span(number, source), span(number, source), {"occ": partner, "vir": vir})
@@ -155,7 +215,7 @@
             for k in range(per_slot):
                 pieces = []
                 for s in range(slots):
-                    at = tab_smem[group, r, k, s]
+                    at = tab_smem[group, r, s, k]
                     if spread:
                         at = at - y * (CORES * tiles)
                         good = (at >= 0) & (at < CORES * tiles)
@@ -268,21 +328,7 @@
     chunks = CHUNKS if ny == 2 else tuple((False, first, width) for _, first, width in CHUNKS)
     jobs = jobs_of(ny, chunks)
 
-    here = amp_slots[0]
-    store = (jnp.arange(slots, dtype=jnp.int32) // per_owner) * owned + here
-    hot = store[:, None] == jnp.arange(nv * owned, dtype=jnp.int32)[None, :]
-    tile_id = jnp.sum(jnp.where(hot, slot_tile[None, :], 0), axis=1)
-    columns = jnp.sum(jnp.where(hot[:, :, None], int_columns[None], 0), axis=1)
-    entry = jnp.arange(share * no, dtype=jnp.int32)
-    place = (entry // share) * tiles + entry % share
-    match = columns[:, :, None] == tile_id[None, None, :]
-    place = place[None, :, None] + (here * share)[:, None, None]
-    table = jnp.min(jnp.where(match, place, no * tiles), axis=1)
-    table = table.reshape(nv, per_owner, slots)
-    table = jnp.pad(table, ((0, 0), (0, 8 - per_owner), (0, 128 - slots)))
-
-    amps = jnp.swapaxes(amplitudes[0], 1, 2).reshape(nv, per_owner * tile, tile)
-    ints = jnp.swapaxes(integrals, 2, 3).reshape(tiles, tile, tile)
+    ints = integrals.reshape(tiles, tile, tile)
 
     bf16 = jnp.bfloat16
     groups = ny if any(c[0] for c in chunks) else 1
@@ -299,23 +345,33 @@
         for w, (_, step) in zip(widths, jobs)
     ]
     scratch += [
+        pltpu.VMEM((min(4, owned) * share, tile, tile), bf16),
+        pltpu.VMEM((slots, tile, tile), bf16),
+        pltpu.VMEM((nv, per_owner * tile, tile), bf16),
+        pltpu.VMEM((nv, slots, 128), jnp.int32),
         pltpu.VMEM((groups, nv, per_owner * tile, tile), bf16),
-        pltpu.VMEM((groups, nv, 8, 128), jnp.int32),
-        pltpu.SMEM((groups, nv, 8, 128), jnp.int32),
+        pltpu.VMEM((groups, nv, slots, 128), jnp.int32),
+        pltpu.SMEM((groups, nv, slots, 128), jnp.int32),
         pltpu.SemaphoreType.DMA((128,)),
         pltpu.SemaphoreType.DMA((128,)),
-        pltpu.SemaphoreType.DMA((16,)),
+        pltpu.SemaphoreType.DMA((32,)),
     ]
     result = pl.pallas_call(
-        functools.partial(kernel, (ny, nz, nx, slots, tiles), chunks, jobs),
+        functools.partial(kernel, (ny, nz, nx, slots, owned, share), chunks, jobs),
         out_shape=jax.ShapeDtypeStruct((slots, tile, tile), bf16),
-        in_specs=[pl.BlockSpec(memory_space=pl.ANY)] * 3,
+        in_specs=[
+            pl.BlockSpec(memory_space=pltpu.SMEM),
+            pl.BlockSpec(memory_space=pltpu.SMEM),
+            pl.BlockSpec(memory_space=pltpu.VMEM),
+            pl.BlockSpec(memory_space=pl.ANY),
+            pl.BlockSpec(memory_space=pl.ANY),
+        ],
         out_specs=pl.BlockSpec(memory_space=pltpu.VMEM),
         scratch_shapes=scratch,
         compiler_params=pltpu.CompilerParams(
             collective_id=0, has_side_effects=True, vmem_limit_bytes=66_000_000
         ),
-    )(amps, table, ints)
+    )(amp_slots, slot_tile, int_columns, amplitudes[0], ints)
     return jnp.swapaxes(result, 1, 2)[None]
 
 

time: 118 us -> 114 us (0.966)
  the two profiles are of different devices: /device:TPU:0 before, /device:TPU:22 now
where the time goes in v2:
time: 114 us; the launch traced here: 113 us
  Pallas kernels  110 us (96%)
  local copies, waits for them, and re-layouts  3.48 us (3%)
    pallas_call x1, Pallas kernels, body(): pl.pallas_call(functools.partial(kernel, (ny, nz, nx, slots, owned, share...  110 us

profile of v2, /device:TPU:22, one launch (start us, length us, event | category | flops | bytes accessed | tf_op | source)
XLA Modules:
  0.0 113.3 jit_solution(3553019042304747328)
XLA Ops:
  0.0 1.4 %copy.6.columns_of = s32[64,48]{1,0:T(8,128)} copy(s32[64,48]{0,1:T(8,128)} %param.8) | data formatting | bytes 24576 | tf_op args[3]
  1.4 109.9 %shard_map.55 = bf16[16,128,128]{2,1,0:T(8,128)(2,1)} custom-call(s32[1,16]{1,0:T(1,128)} %own_slots.1, s32[64]{0:T(128)} %slot_tile.1, s32[64,48]{1,0:T(8,128)} %copy.6.columns_of, bf16[16,128,128]{2,1,0:T(8,128)(2,1)} %bitcast.7, bf16[96,128,128]{2,1,0:T(8,128)(2,1)} %bitcast.5), custom_call_target="tpu_custom_call" | custom-call | tf_op jit(solution)/shard_map/pallas_call | solution.py:359
  111.3 2.0 %copy.7 = bf16[1,16,128,128]{3,2,1,0:T(8,128)(2,1)} copy(bf16[1,16,128,128]{2,3,1,0:T(8,128)(2,1)} %bitcast.6) | data formatting | bytes 1048576 | tf_op jit(solution)/shard_map/broadcast_in_dim | solution.py:375

commit v3 on v2

--- a/solution.py
+++ b/solution.py
@@ -9,7 +9,7 @@
 
 MESH = pl.DeviceIdType.MESH
 CORES = 2
-CHUNKS = ((False, 0, 32), (False, 32, 32), (False, 64, 32), (False, 96, 16), (False, 112, 16))
+CHUNKS = tuple((False, 16 * i, 16) for i in range(8))
 
 
 def jobs_of(ny, chunks):
@@ -20,7 +20,20 @@
     return jobs
 
 
-def kernel(dims, chunks, jobs, own_slots, slot_tile, columns_of, amps_in, ints, out, *scratch):
+def events_of(chunks, jobs):
+    spread = [j for j, (c, _) in enumerate(jobs) if chunks[c][0]]
+    plain = [j for j, (c, _) in enumerate(jobs) if not chunks[c][0]]
+    order = spread[:1] + plain[:1] + spread[1:] + plain[1:]
+    events = []
+    count = len(order)
+    for at in range(count + 2):
+        for stage, back in ((1, 0), (2, 1), (3, 2)):
+            if 0 <= at - back < count and not (stage == 3 and order[at - back] in spread[:1]):
+                events.append((stage, order[at - back]))
+    return events + [(3, one) for one in spread[:1]]
+
+
+def kernel(dims, chunks, jobs, events, own_slots, slot_tile, columns_of, amps_in, ints, out, *scratch):
     ny, nz, nx, slots, owned, share = dims
     tiles = owned * share
     nv, no = nz * nx, ny * CORES
@@ -279,41 +292,22 @@
                 total += from_y[other][...].astype(jnp.float32)
         out[:, pl.ds(first, width), :] = total.astype(jnp.bfloat16)
 
-    if spread_any:
-        order = [j for j in range(n_jobs) if jobs[j][1] == 0 and chunks[jobs[j][0]][0]]
-        order += [j for j in range(n_jobs) if not chunks[jobs[j][0]][0]]
-        late = [j for j in range(n_jobs) if jobs[j][1] > 0]
-        order = order[:2] + late + order[2:]
-    else:
-        order = list(range(n_jobs))
     gathered = set()
-    finals = []
-
-    def flush(job):
-        if chunks[jobs[job][0]][0] and jobs[job][1] == 0:
-            finals.append(job)
+    for stage, job in events:
+        number, step = jobs[job]
+        if stage == 1:
+            if number not in gathered:
+                gathered.add(number)
+                gather(number)
+            if step > 0:
+                for copy in others[step - 1]:
+                    copy.wait_recv()
+                local(tab_buf.at[step], tab_smem.at[step]).wait()
+            first_stage(job)
+        elif stage == 2:
+            second_stage(job)
         else:
             third_stage(job)
-
-    previous = None
-    for job in order:
-        number, step = jobs[job]
-        if number not in gathered:
-            gathered.add(number)
-            gather(number)
-        if step > 0:
-            for copy in others[step - 1]:
-                copy.wait_recv()
-            again = local(tab_buf.at[step], tab_smem.at[step])
-            again.wait()
-        first_stage(job)
-        if previous is not None:
-            flush(previous)
-        second_stage(job)
-        previous = job
-    flush(previous)
-    for job in finals:
-        third_stage(job)
     for copy in sent:
         copy.wait_send()
 
@@ -357,7 +351,7 @@
         pltpu.SemaphoreType.DMA((32,)),
     ]
     result = pl.pallas_call(
-        functools.partial(kernel, (ny, nz, nx, slots, owned, share), chunks, jobs),
+        functools.partial(kernel, (ny, nz, nx, slots, owned, share), chunks, jobs, events_of(chunks, jobs)),
         out_shape=jax.ShapeDtypeStruct((slots, tile, tile), bf16),
         in_specs=[
             pl.BlockSpec(memory_space=pltpu.SMEM),

time: 114 us -> 101 us (0.89)
  the two profiles are of different devices: /device:TPU:22 before, /device:TPU:0 now
where the time goes in v3:
time: 101 us; the launch traced here: 100 us
  Pallas kernels  96.8 us (96%)
  local copies, waits for them, and re-layouts  3.48 us (3%)
    pallas_call x1, Pallas kernels, body(): pl.pallas_call(functools.partial(kernel, (ny, nz, nx, slots, owned, share...  96.8 us
    broadcast_in_dim x1, local copies, waits for them, and re-layouts, body(): return jnp.swapaxes(result, 1, 2)[None]  2.04 us

profile of v3, /device:TPU:0, one launch (start us, length us, event | category | flops | bytes accessed | tf_op | source)
XLA Modules:
  0.0 100.2 jit_solution(15466296593273346648)
XLA Ops:
  0.0 1.4 %copy.6.columns_of = s32[64,48]{1,0:T(8,128)} copy(s32[64,48]{0,1:T(8,128)} %param.8) | data formatting | bytes 24576 | tf_op args[3]
  1.4 96.8 %shard_map.55 = bf16[16,128,128]{2,1,0:T(8,128)(2,1)} custom-call(s32[1,16]{1,0:T(1,128)} %own_slots.1, s32[64]{0:T(128)} %slot_tile.1, s32[64,48]{1,0:T(8,128)} %copy.6.columns_of, bf16[16,128,128]{2,1,0:T(8,128)(2,1)} %bitcast.7, bf16[96,128,128]{2,1,0:T(8,128)(2,1)} %bitcast.5), custom_call_target="tpu_custom_call" | custom-call | tf_op jit(solution)/shard_map/pallas_call | solution.py:353
  98.2 2.0 %copy.7 = bf16[1,16,128,128]{3,2,1,0:T(8,128)(2,1)} copy(bf16[1,16,128,128]{2,3,1,0:T(8,128)(2,1)} %bitcast.6) | data formatting | bytes 1048576 | tf_op jit(solution)/shard_map/broadcast_in_dim | solution.py:369
